TPU v7x, 32 devices: a whole 2x2x4 slice. The times are simulated.
32 devices in a mesh: dp: 4 (over y, x), expert: 8 (over z, core).
Axes of the slice: x: 2, y: 2, z: 4, core: 2. Of those that a mesh axis runs over, the one named last changes fastest.
Arguments:
- features: float32 [32768, 256], P(('dp', 'expert')), may hold values from -6 to 6
- cotangent: float32 [32768, 512], P(('dp', 'expert')), may hold values from -6 to 6
- routes: int32 [32768, 8], P(('dp', 'expert')), may hold values from 0 to 15, all different within a row; in each aligned block of 256 rows (0 to 255, 256 to 511, ...) at most 192 rows name the same one
- lengths: int32 [32, 16], P(('dp', 'expert')), may hold values from 1 to 200, 1024 in all within a row
- gate_weight: float32 [256, 40], replicated, may hold values from -0.1875 to 0.1875
- first_weight: float32 [16, 256, 256], P('expert', 'dp'), may hold values from -0.375 to 0.375
- second_weight: float32 [16, 256, 256], P('expert', 'dp'), may hold values from -0.75 to 0.75
- expert_bias: float32 [16, 512], P('expert', 'dp'), may hold values from -0.625 to 0.625
- gate_momentum: float32 [256, 40], replicated, may hold values from -12 to 12
- gate_average: float32 [256, 40], replicated, may hold values from -0.1875 to 0.1875
- first_momentum: float32 [16, 256, 256], P('expert', 'dp'), may hold values from -1.25 to 1.25
- first_average: float32 [16, 256, 256], P('expert', 'dp'), may hold values from -0.375 to 0.375
- second_momentum: float32 [16, 256, 256], P('expert', 'dp'), may hold values from -0.625 to 0.625
- second_average: float32 [16, 256, 256], P('expert', 'dp'), may hold values from -0.75 to 0.75
- bias_momentum: float32 [16, 512], P('expert', 'dp'), may hold values from -1.25 to 1.25
- bias_average: float32 [16, 512], P('expert', 'dp'), may hold values from -0.625 to 0.625
Outputs:
- task_outputs: float32 [32768, 512], P(('dp', 'expert'))
- input_grad: float32 [32768, 256], P(('dp', 'expert'))
- gate_momentum_new: float32 [256, 40], replicated
- gate_weight_new: float32 [256, 40], replicated
- gate_average_new: float32 [256, 40], replicated
- first_momentum_new: float32 [16, 256, 256], P('expert', 'dp')
- first_weight_new: float32 [16, 256, 256], P('expert', 'dp')
- first_average_new: float32 [16, 256, 256], P('expert', 'dp')
- second_momentum_new: float32 [16, 256, 256], P('expert', 'dp')
- second_weight_new: float32 [16, 256, 256], P('expert', 'dp')
- second_average_new: float32 [16, 256, 256], P('expert', 'dp')
- bias_momentum_new: float32 [16, 512], P('expert', 'dp')
- bias_new: float32 [16, 512], P('expert', 'dp')
- bias_average_new: float32 [16, 512], P('expert', 'dp')
Inputs may be any that keep to these rules, and one draw needn't show every extreme that they name: `routes`: each row names 8 different experts: the first 4 are task 0's selectors, the next 4 task 1's. In each aligned block of 256 rows (one micro-batch of one device) no expert is named by more than 192 rows, and in some block one expert is named by exactly 192 rows. `lengths`: the sessions of one device cover its 1024 rows in order and never cross devices; the longest has the maximum length.
All inputs are finite; a program needn't handle non-finite values.
Results may differ from a plain program's by a relative error of at most 0.002.
Values sent between devices are 32-bit elements; how exact they have to be, the bound alone decides.
A program may use at most 192 MiB of HBM per device.

v0:
```python
import math

import jax
import jax.numpy as jnp
from jax import lax
from jax.sharding import PartitionSpec as P

D = 256
HID = 256
DOUT = 256
EXPERTS = 16
BITS = 4
TASKS = 2
SELECT = 4
MICRO = 4
CAP = 192


HIGHEST = lax.Precision.HIGHEST
OFFSET = 3.5
SHARPNESS = 10.0
MOMENTUM = 0.5
AVERAGE_DECAY = 0.5
EXPERT_RATE = 0.4
GATE_RATE = 0.01


def smooth_step(argument):
    clipped = jnp.clip(argument, -0.5 * SHARPNESS, 0.5 * SHARPNESS)
    return -2.0 / SHARPNESS**3 * clipped**3 + 1.5 / SHARPNESS * clipped + 0.5


def gate_strengths(features, gate_weight, lengths_row, chosen):
    row_count = features.shape[0]
    session_ends = jnp.cumsum(lengths_row, dtype=jnp.int32)
    starts = session_ends - lengths_row
    places = jnp.arange(row_count, dtype=jnp.int32)[:, None]
    member = ((places >= starts[None, :]) & (places < session_ends[None, :])).astype(jnp.float32)
    session_sums = jnp.dot(member.T, features, precision=HIGHEST)
    session_means = session_sums / lengths_row.astype(jnp.float32)[:, None]
    context = features + jnp.dot(member, session_means, precision=HIGHEST)
    logits = jnp.dot(context, gate_weight, precision=HIGHEST).reshape(
        row_count, TASKS, SELECT, BITS + 1
    )
    weights = jax.nn.softmax(logits[..., 0], axis=-1)
    powers = 2 ** jnp.arange(BITS, dtype=jnp.int32)
    code_bits = chosen.reshape(row_count, TASKS, SELECT)[..., None] // powers % 2
    code_signs = 2.0 * code_bits.astype(jnp.float32) - 1.0
    strength = jnp.prod(smooth_step(code_signs * logits[..., 1:] + OFFSET), axis=-1)
    return (weights * strength).reshape(row_count, TASKS * SELECT)


def slot_index(chosen):
    destination = chosen.reshape(-1)
    matches = (destination[:, None] == jnp.arange(EXPERTS, dtype=jnp.int32)[None, :]).astype(
        jnp.int32
    )
    before = jnp.cumsum(matches, axis=0, dtype=jnp.int32) - matches
    position = jnp.sum(before * matches, axis=1, dtype=jnp.int32)
    return destination * CAP + position


def expert_forward(slot_rows, first_full, second_full, bias_full):
    pre_act = (
        jnp.einsum("sjcd,jdh->sjch", slot_rows, first_full, precision=HIGHEST)
        + bias_full[None, :, None, :HID]
    )
    hidden = jax.nn.relu(pre_act)
    slot_out = (
        jnp.einsum("sjch,jho->sjco", hidden, second_full, precision=HIGHEST)
        + bias_full[None, :, None, HID:]
    )
    return (pre_act, hidden, slot_out)


def expert_backward(slot_rows, pre_act, hidden, slot_cot, first_full, second_full):
    second_delta = jnp.einsum("sjch,sjco->jho", hidden, slot_cot, precision=HIGHEST)
    hidden_cot = jnp.einsum("sjco,jho->sjch", slot_cot, second_full, precision=HIGHEST) * (
        pre_act > 0.0
    ).astype(jnp.float32)
    first_delta = jnp.einsum("sjcd,sjch->jdh", slot_rows, hidden_cot, precision=HIGHEST)
    bias_delta = jnp.concatenate(
        [jnp.sum(hidden_cot, axis=(0, 2)), jnp.sum(slot_cot, axis=(0, 2))], axis=-1
    )
    slot_back = jnp.einsum("sjch,jdh->sjcd", hidden_cot, first_full, precision=HIGHEST)
    return (slot_back, (first_delta, second_delta, bias_delta))


def apply_update(weight, gradient, momentum, average, step_rate):
    momentum_new = MOMENTUM * momentum + gradient
    weight_new = weight - step_rate * (gradient + MOMENTUM * momentum_new)
    average_new = AVERAGE_DECAY * average + (1.0 - AVERAGE_DECAY) * weight_new
    return (momentum_new, weight_new, average_new)


def local(
    features,
    cotangent,
    routes,
    lengths,
    gate_weight,
    first_weight,
    second_weight,
    expert_bias,
    gate_momentum,
    gate_average,
    first_momentum,
    first_average,
    second_momentum,
    second_average,
    bias_momentum,
    bias_average,
):
    row_count = features.shape[0]
    pair_count = TASKS * SELECT
    micro_rows = row_count // MICRO

    def gate_part(rows_in, weight_in):
        return gate_strengths(rows_in, weight_in, lengths[0], routes)

    gate_terms, gate_pull = jax.vjp(gate_part, features, gate_weight)
    pair_cot = jnp.broadcast_to(
        cotangent.reshape(row_count, TASKS, 1, DOUT), (row_count, TASKS, SELECT, DOUT)
    ).reshape(row_count, pair_count, DOUT)
    pair_grads = gate_terms[:, :, None] * pair_cot
    local_count = first_weight.shape[0]
    first_sum = jnp.zeros((local_count, D, HID), jnp.float32)
    second_sum = jnp.zeros((local_count, HID, DOUT), jnp.float32)
    bias_sum = jnp.zeros((local_count, HID + DOUT), jnp.float32)
    output_parts = []
    input_parts = []
    cot_parts = []
    for micro_index in range(MICRO):
        begin = micro_index * micro_rows
        first_full = lax.all_gather(first_weight, "dp", axis=1, tiled=True)
        second_full = lax.all_gather(second_weight, "dp", axis=1, tiled=True)
        bias_full = lax.all_gather(expert_bias, "dp", axis=1, tiled=True)
        rows_now = features[begin : begin + micro_rows]
        slot_place = slot_index(routes[begin : begin + micro_rows])
        send_rows = (
            jnp.zeros((EXPERTS * CAP, D), jnp.float32)
            .at[slot_place]
            .set(jnp.repeat(rows_now, pair_count, axis=0))
            .reshape(EXPERTS, CAP, D)
        )
        send_grads = (
            jnp.zeros((EXPERTS * CAP, DOUT), jnp.float32)
            .at[slot_place]
            .set(pair_grads[begin : begin + micro_rows].reshape(-1, DOUT))
            .reshape(EXPERTS, CAP, DOUT)
        )
        got_rows = lax.all_to_all(send_rows, "expert", split_axis=0, concat_axis=0, tiled=True)
        slot_rows = got_rows.reshape(-1, local_count, CAP, D)
        pre_act, hidden, slot_out = expert_forward(slot_rows, first_full, second_full, bias_full)
        returned_out = lax.all_to_all(
            slot_out.reshape(EXPERTS, CAP, DOUT), "expert", split_axis=0, concat_axis=0, tiled=True
        )
        got_grads = lax.all_to_all(send_grads, "expert", split_axis=0, concat_axis=0, tiled=True)
        slot_back, deltas = expert_backward(
            slot_rows,
            pre_act,
            hidden,
            got_grads.reshape(-1, local_count, CAP, DOUT),
            first_full,
            second_full,
        )
        returned_back = lax.all_to_all(
            slot_back.reshape(EXPERTS, CAP, D), "expert", split_axis=0, concat_axis=0, tiled=True
        )
        first_sum = first_sum + deltas[0]
        second_sum = second_sum + deltas[1]
        bias_sum = bias_sum + deltas[2]
        picked = returned_out.reshape(EXPERTS * CAP, DOUT)[slot_place].reshape(
            micro_rows, TASKS, SELECT, DOUT
        )
        combined = jnp.sum(
            gate_terms[begin : begin + micro_rows].reshape(micro_rows, TASKS, SELECT, 1) * picked,
            axis=2,
        )
        output_parts.append(combined.reshape(micro_rows, TASKS * DOUT))
        cot_parts.append(
            jnp.sum(
                pair_cot[begin : begin + micro_rows] * picked.reshape(micro_rows, pair_count, DOUT),
                axis=-1,
            )
        )
        input_parts.append(
            jnp.sum(
                returned_back.reshape(EXPERTS * CAP, D)[slot_place].reshape(
                    micro_rows, pair_count, D
                ),
                axis=1,
            )
        )
    task_outputs = jnp.concatenate(output_parts, axis=0)
    rows_from_gate, gate_local = gate_pull(jnp.concatenate(cot_parts, axis=0))
    input_grad = rows_from_gate + jnp.concatenate(input_parts, axis=0)
    gate_grad = lax.psum(gate_local, ("dp", "expert"))
    first_grad, second_grad, bias_grad = (
        lax.psum_scatter(first_sum, "dp", scatter_dimension=1, tiled=True),
        lax.psum_scatter(second_sum, "dp", scatter_dimension=1, tiled=True),
        lax.psum_scatter(bias_sum, "dp", scatter_dimension=1, tiled=True),
    )
    grad_scale = 1.0 / math.sqrt(row_count * lax.axis_size("dp") * lax.axis_size("expert"))
    gate_new = apply_update(
        gate_weight, gate_grad * grad_scale, gate_momentum, gate_average, GATE_RATE
    )
    first_new = apply_update(
        first_weight, first_grad * grad_scale, first_momentum, first_average, EXPERT_RATE
    )
    second_new = apply_update(
        second_weight, second_grad * grad_scale, second_momentum, second_average, EXPERT_RATE
    )
    bias_new = apply_update(
        expert_bias, bias_grad * grad_scale, bias_momentum, bias_average, EXPERT_RATE
    )
    return (
        task_outputs,
        input_grad,
        gate_new[0],
        gate_new[1],
        gate_new[2],
        first_new[0],
        first_new[1],
        first_new[2],
        second_new[0],
        second_new[1],
        second_new[2],
        bias_new[0],
        bias_new[1],
        bias_new[2],
    )


def solution(mesh):
    placed = (
        P(("dp", "expert"), None),
        P(("dp", "expert"), None),
        P(("dp", "expert"), None),
        P(("dp", "expert"), None),
        P(),
        P("expert", "dp", None),
        P("expert", "dp", None),
        P("expert", "dp"),
        P(),
        P(),
        P("expert", "dp", None),
        P("expert", "dp", None),
        P("expert", "dp", None),
        P("expert", "dp", None),
        P("expert", "dp"),
        P("expert", "dp"),
    )
    return jax.shard_map(
        local,
        mesh=mesh,
        in_specs=placed,
        out_specs=(
            P(("dp", "expert"), None),
            P(("dp", "expert"), None),
            P(),
            P(),
            P(),
            P("expert", "dp", None),
            P("expert", "dp", None),
            P("expert", "dp", None),
            P("expert", "dp", None),
            P("expert", "dp", None),
            P("expert", "dp", None),
            P("expert", "dp"),
            P("expert", "dp"),
            P("expert", "dp"),
        ),
        check_vma=False,
    )
```

profile of v0, /device:TPU:0, one launch (start us, length us, event | category | flops | bytes accessed | tf_op | source)
XLA Modules:
  0.0 1447.1 jit_solution(313344892652982760)
XLA Ops:
  16.6 10.9 scatter_custom_fusion
  27.5 6.3 all-to-all-start
  37.5 8.1 reduce-window.41
  53.4 11.3 scatter_custom_fusion.3
  64.7 40.7 %all-to-all-done = f32[16,192,256]{2,1,0:T(8,128)S(1)} async-done(((f32[16,192,256]{2,1,0:T(8,128)}), f32[16,192,256]{2,1,0:T(8,128)S(1)}, u32[]{:S(2)}, u32[]{:S(2)}) %all-to-all-start) | async-done | bytes 3145760 | tf_op jit(solution)/shard_map/all_to_all | solution.py:152
  114.4 8.1 reduce-window.39
  130.3 11.2 scatter_custom_fusion.2
  141.6 40.6 %all-to-all-done.6 = f32[16,192,256]{2,1,0:T(8,128)S(1)} async-done(((f32[16,192,256]{2,1,0:T(8,128)}), f32[16,192,256]{2,1,0:T(8,128)S(1)}, u32[]{:S(2)}, u32[]{:S(2)}) %all-to-all-start.6) | async-done | bytes 3145760 | tf_op jit(solution)/shard_map/all_to_all | solution.py:152
  183.9 4.7 all-to-all-start.4
  194.5 10.9 scatter_custom_fusion.1
  205.4 54.6 %all-to-all-done.4 = f32[16,192,256]{2,1,0:T(8,128)} async-done(((f32[16,192,256]{2,1,0:T(8,128)}), f32[16,192,256]{2,1,0:T(8,128)}, u32[]{:S(2)}, u32[]{:S(2)}) %all-to-all-start.4) | async-done | bytes 3145760 | tf_op jit(solution)/shard_map/all_to_all | solution.py:152
  263.9 8.1 all_gather.7
  272.0 10.7 all_gather.6
  282.7 9.2 all_gather.8
  291.9 5.1 fusion.30
  302.2 33.1 %all-to-all-done.2 = f32[16,192,256]{2,1,0:T(8,128)S(1)} async-done(((f32[16,192,256]{2,1,0:T(8,128)}), f32[16,192,256]{2,1,0:T(8,128)S(1)}, u32[]{:S(2)}, u32[]{:S(2)}) %all-to-all-start.2) | async-done | bytes 3145760 | tf_op jit(solution)/shard_map/all_to_all | solution.py:152
  340.9 5.1 fusion.24
  351.1 61.2 %all-to-all-done.1 = f32[16,192,256]{2,1,0:T(8,128)S(1)} async-done(((f32[16,192,256]{2,1,0:T(8,128)}), f32[16,192,256]{2,1,0:T(8,128)S(1)}, u32[]{:S(2)}, u32[]{:S(2)}) %all-to-all-start.1) | async-done | bytes 3145760 | tf_op jit(solution)/shard_map/all_to_all | solution.py:155
  412.3 4.9 all-to-all-start.7
  417.3 5.1 fusion.26
  427.6 61.2 %all-to-all-done.7 = f32[16,192,256]{2,1,0:T(8,128)} async-done(((f32[16,192,256]{2,1,0:T(8,128)}), f32[16,192,256]{2,1,0:T(8,128)}, u32[]{:S(2)}, u32[]{:S(2)}) %all-to-all-start.7) | async-done | bytes 3145760 | tf_op jit(solution)/shard_map/all_to_all | solution.py:155
  488.8 4.6 all-to-all-start.5
  493.4 5.1 fusion.28
  503.7 61.3 %all-to-all-done.5 = f32[16,192,256]{2,1,0:T(8,128)} async-done(((f32[16,192,256]{2,1,0:T(8,128)}), f32[16,192,256]{2,1,0:T(8,128)}, u32[]{:S(2)}, u32[]{:S(2)}) %all-to-all-start.5) | async-done | bytes 3145760 | tf_op jit(solution)/shard_map/all_to_all | solution.py:155
  565.0 4.8 all-to-all-start.3
  617.9 6.2 broadcast_in_dim.98
  624.1 10.2 reshape.768
  641.1 9.3 gather_fusion
  653.6 8.5 gather_fusion.3
  665.4 10.4 gather_fusion.2
  679.0 8.5 gather_fusion.1
  692.6 6.1 broadcast_multiply_fusion
  698.7 11.5 scatter_custom_fusion.7
  710.2 5.6 all-to-all-start.14
  715.7 11.5 scatter_custom_fusion.6
  727.2 60.0 %all-to-all-done.14 = f32[16,192,256]{2,1,0:T(8,128)S(1)} async-done(((f32[16,192,256]{2,1,0:T(8,128)}), f32[16,192,256]{2,1,0:T(8,128)S(1)}, u32[]{:S(2)}, u32[]{:S(2)}) %all-to-all-start.14) | async-done | bytes 3145760 | tf_op jit(solution)/shard_map/all_to_all | solution.py:158
  793.5 11.4 scatter_custom_fusion.5
  804.9 60.1 %all-to-all-done.12 = f32[16,192,256]{2,1,0:T(8,128)} async-done(((f32[16,192,256]{2,1,0:T(8,128)}), f32[16,192,256]{2,1,0:T(8,128)}, u32[]{:S(2)}, u32[]{:S(2)}) %all-to-all-start.12) | async-done | bytes 3145760 | tf_op jit(solution)/shard_map/all_to_all | solution.py:158
  868.7 11.5 scatter_custom_fusion.4
  880.2 60.0 %all-to-all-done.10 = f32[16,192,256]{2,1,0:T(8,128)S(1)} async-done(((f32[16,192,256]{2,1,0:T(8,128)}), f32[16,192,256]{2,1,0:T(8,128)S(1)}, u32[]{:S(2)}, u32[]{:S(2)}) %all-to-all-start.10) | async-done | bytes 3145760 | tf_op jit(solution)/shard_map/all_to_all | solution.py:158
  941.8 4.9 all-to-all-start.8
  946.7 5.7 fusion.255
  957.4 60.8 %all-to-all-done.8 = f32[16,192,256]{2,1,0:T(8,128)} async-done(((f32[16,192,256]{2,1,0:T(8,128)}), f32[16,192,256]{2,1,0:T(8,128)}, u32[]{:S(2)}, u32[]{:S(2)}) %all-to-all-start.8) | async-done | bytes 3145760 | tf_op jit(solution)/shard_map/all_to_all | solution.py:158
  1022.1 6.8 fusion.254
  1033.9 59.7 %all-to-all-done.15 = f32[16,192,256]{2,1,0:T(8,128)S(1)} async-done(((f32[16,192,256]{2,1,0:T(8,128)}), f32[16,192,256]{2,1,0:T(8,128)S(1)}, u32[]{:S(2)}, u32[]{:S(2)}) %all-to-all-start.15) | async-done | bytes 3145760 | tf_op jit(solution)/shard_map/all_to_all | solution.py:167
  1093.5 4.7 all-to-all-start.13
  1098.2 6.7 fusion.253
  1110.0 59.8 %all-to-all-done.13 = f32[16,192,256]{2,1,0:T(8,128)} async-done(((f32[16,192,256]{2,1,0:T(8,128)}), f32[16,192,256]{2,1,0:T(8,128)}, u32[]{:S(2)}, u32[]{:S(2)}) %all-to-all-start.13) | async-done | bytes 3145760 | tf_op jit(solution)/shard_map/all_to_all | solution.py:167
  1169.7 4.9 all-to-all-start.11
  1243.9 41.1 %psum.7 = f32[256,40]{0,1:T(8,128)S(1)} all-reduce(f32[256,40]{0,1:T(8,128)S(1)} %fusion.258), channel_id=1, replica_groups=mesh['dp'=4,'expert'=8] {'dp','expert'}, use_global_device_ids=true, to_apply=%region_36.37 | all-reduce | flops 10240 | bytes 81920 | tf_op jit(solution)/shard_map/psum | solution.py:198
  1285.0 6.2 fusion.252
  1311.5 8.2 fusion.125
  1319.7 5.2 fusion.164
  1325.0 7.7 fusion.159
  1332.7 6.0 fusion.154
  1339.0 8.1 fusion.113
  1347.1 5.2 fusion.151
  1352.3 7.4 fusion.148
  1359.8 6.0 fusion.145
  1374.8 17.6 %reduce-scatter.6.cloned.1.call-done = f32[2,64,256]{2,1,0:T(8,128)} async-done(((f32[2,256,256]{2,1,0:T(8,128)}), f32[2,64,256]{2,1,0:T(8,128)}) %reduce-scatter.6.cloned.1.call-update) | async-done | bytes 131088 | tf_op jit(solution)/shard_map/reduce_scatter | solution.py:200
  1394.3 8.8 gather_fusion.7
  1403.2 10.5 gather_fusion.6
  1413.6 10.6 gather_fusion.5
  1428.4 8.6 gather_fusion.4
  (389 shorter events, 282.3 us)
Async XLA Ops:
  16.6 10.9 copy-start.69
  27.5 77.9 %all-to-all-start = ((f32[16,192,256]{2,1,0:T(8,128)}), f32[16,192,256]{2,1,0:T(8,128)S(1)}, u32[]{:S(2)}, u32[]{:S(2)}) async-start(f32[16,192,256]{2,1,0:T(8,128)} %bitcast.394), calls=%async_computation | async-start | bytes 6291456 | tf_op jit(solution)/shard_map/all_to_all | solution.py:152
  53.4 53.7 %copy-start.71 = (s32[2048,1]{0,1:T(1,128)}, s32[2048,1]{0,1:T(1,128)S(1)}, u32[]{:S(2)}) copy-start(s32[2048,1]{0,1:T(1,128)S(1)} %compare_select_fusion) | copy-start | bytes 24580
  107.1 75.1 %all-to-all-start.6 = ((f32[16,192,256]{2,1,0:T(8,128)}), f32[16,192,256]{2,1,0:T(8,128)S(1)}, u32[]{:S(2)}, u32[]{:S(2)}) async-start(f32[16,192,256]{2,1,0:T(8,128)} %bitcast.393), calls=%async_computation.6 | async-start | bytes 6291456 | tf_op jit(solution)/shard_map/all_to_all | solution.py:152
  130.3 51.9 %copy-start.73 = (s32[2048,1]{0,1:T(1,128)}, s32[2048,1]{0,1:T(1,128)S(1)}, u32[]{:S(2)}) copy-start(s32[2048,1]{0,1:T(1,128)S(1)} %compare_select_fusion.1) | copy-start | bytes 24580
  183.9 76.2 %all-to-all-start.4 = ((f32[16,192,256]{2,1,0:T(8,128)}), f32[16,192,256]{2,1,0:T(8,128)}, u32[]{:S(2)}, u32[]{:S(2)}) async-start(f32[16,192,256]{2,1,0:T(8,128)} %bitcast.392), calls=%async_computation.4 | async-start | bytes 6291456 | tf_op jit(solution)/shard_map/all_to_all | solution.py:152
  194.5 65.6 %copy-start.75 = (s32[2048,1]{0,1:T(1,128)}, s32[2048,1]{0,1:T(1,128)S(1)}, u32[]{:S(2)}) copy-start(s32[2048,1]{0,1:T(1,128)S(1)} %compare_select_fusion.2) | copy-start | bytes 24580
  260.1 11.9 copy-start.45
  260.1 22.6 %copy-start.43 = (f32[2,64,256]{2,1,0:T(8,128)S(1)}, f32[2,64,256]{2,1,0:T(8,128)}, u32[]{:S(2)}) copy-start(f32[2,64,256]{2,1,0:T(8,128)} %param.22) | copy-start | bytes 393220
  260.1 75.3 %all-to-all-start.2 = ((f32[16,192,256]{2,1,0:T(8,128)}), f32[16,192,256]{2,1,0:T(8,128)S(1)}, u32[]{:S(2)}, u32[]{:S(2)}) async-start(f32[16,192,256]{2,1,0:T(8,128)} %bitcast.395), calls=%async_computation.2 | async-start | bytes 6291456 | tf_op jit(solution)/shard_map/all_to_all | solution.py:152
  282.7 14.3 copy-start.16
  291.9 5.2 copy-start.12
  337.0 75.4 %all-to-all-start.1 = ((f32[16,192,256]{2,1,0:T(8,128)}), f32[16,192,256]{2,1,0:T(8,128)S(1)}, u32[]{:S(2)}, u32[]{:S(2)}) async-start(f32[16,192,256]{2,1,0:T(8,128)} %bitcast.399), calls=%async_computation.1 | async-start | bytes 6291456 | tf_op jit(solution)/shard_map/all_to_all | solution.py:155
  412.3 76.5 %all-to-all-start.7 = ((f32[16,192,256]{2,1,0:T(8,128)}), f32[16,192,256]{2,1,0:T(8,128)}, u32[]{:S(2)}, u32[]{:S(2)}) async-start(f32[16,192,256]{2,1,0:T(8,128)} %bitcast.400), calls=%async_computation.7 | async-start | bytes 6291456 | tf_op jit(solution)/shard_map/all_to_all | solution.py:155
  488.8 76.2 %all-to-all-start.5 = ((f32[16,192,256]{2,1,0:T(8,128)}), f32[16,192,256]{2,1,0:T(8,128)}, u32[]{:S(2)}, u32[]{:S(2)}) async-start(f32[16,192,256]{2,1,0:T(8,128)} %bitcast.398), calls=%async_computation.5 | async-start | bytes 6291456 | tf_op jit(solution)/shard_map/all_to_all | solution.py:155
  565.0 114.0 %all-to-all-start.3 = ((f32[16,192,256]{2,1,0:T(8,128)}), f32[16,192,256]{2,1,0:T(8,128)}, u32[]{:S(2)}, u32[]{:S(2)}) async-start(f32[16,192,256]{2,1,0:T(8,128)} %bitcast.391), calls=%async_computation.3 | async-start | bytes 6291456 | tf_op jit(solution)/shard_map/all_to_all | solution.py:155
  569.8 5.5 copy-start.47
  570.7 8.1 copy-start.77
  570.7 8.1 copy-start.82
  578.1 8.4 copy-start.49
  578.1 8.4 copy-start.50
  624.1 10.3 copy-start.70
  624.1 10.9 copy-start.76
  624.1 11.5 copy-start.74
  624.1 12.1 copy-start.72
  634.4 6.0 copy-start.87
  662.1 13.7 copy-start.33
  664.9 11.0 copy-start.53
  678.4 9.1 copy-start.54
  687.6 11.1 copy-start.34
  710.2 77.1 %all-to-all-start.14 = ((f32[16,192,256]{2,1,0:T(8,128)}), f32[16,192,256]{2,1,0:T(8,128)S(1)}, u32[]{:S(2)}, u32[]{:S(2)}) async-start(f32[16,192,256]{2,1,0:T(8,128)} %bitcast.404), calls=%async_computation.14 | async-start | bytes 6291456 | tf_op jit(solution)/shard_map/all_to_all | solution.py:158
  789.0 76.0 %all-to-all-start.12 = ((f32[16,192,256]{2,1,0:T(8,128)}), f32[16,192,256]{2,1,0:T(8,128)}, u32[]{:S(2)}, u32[]{:S(2)}) async-start(f32[16,192,256]{2,1,0:T(8,128)} %bitcast.403), calls=%async_computation.12 | async-start | bytes 6291456 | tf_op jit(solution)/shard_map/all_to_all | solution.py:158
  865.0 75.1 %all-to-all-start.10 = ((f32[16,192,256]{2,1,0:T(8,128)}), f32[16,192,256]{2,1,0:T(8,128)S(1)}, u32[]{:S(2)}, u32[]{:S(2)}) async-start(f32[16,192,256]{2,1,0:T(8,128)} %bitcast.402), calls=%async_computation.10 | async-start | bytes 6291456 | tf_op jit(solution)/shard_map/all_to_all | solution.py:158
  941.8 76.4 %all-to-all-start.8 = ((f32[16,192,256]{2,1,0:T(8,128)}), f32[16,192,256]{2,1,0:T(8,128)}, u32[]{:S(2)}, u32[]{:S(2)}) async-start(f32[16,192,256]{2,1,0:T(8,128)} %bitcast.401), calls=%async_computation.8 | async-start | bytes 6291456 | tf_op jit(solution)/shard_map/all_to_all | solution.py:158
  946.7 5.8 copy-start.17
  1018.2 75.3 %all-to-all-start.15 = ((f32[16,192,256]{2,1,0:T(8,128)}), f32[16,192,256]{2,1,0:T(8,128)S(1)}, u32[]{:S(2)}, u32[]{:S(2)}) async-start(f32[16,192,256]{2,1,0:T(8,128)} %bitcast.396), calls=%async_computation.15 | async-start | bytes 6291456 | tf_op jit(solution)/shard_map/all_to_all | solution.py:167
  1022.1 6.8 copy-start.18
  1093.5 76.2 %all-to-all-start.13 = ((f32[16,192,256]{2,1,0:T(8,128)}), f32[16,192,256]{2,1,0:T(8,128)}, u32[]{:S(2)}, u32[]{:S(2)}) async-start(f32[16,192,256]{2,1,0:T(8,128)} %bitcast.397), calls=%async_computation.13 | async-start | bytes 6291456 | tf_op jit(solution)/shard_map/all_to_all | solution.py:167
  1098.2 6.8 copy-start.19
  1169.7 126.5 %all-to-all-start.11 = ((f32[16,192,256]{2,1,0:T(8,128)}), f32[16,192,256]{2,1,0:T(8,128)}, u32[]{:S(2)}, u32[]{:S(2)}) async-start(f32[16,192,256]{2,1,0:T(8,128)} %bitcast.390), calls=%async_computation.11 | async-start | bytes 6291456 | tf_op jit(solution)/shard_map/all_to_all | solution.py:167
  1285.0 6.2 copy-start.20
  1296.3 132.1 %all-to-all-start.9 = ((f32[16,192,256]{2,1,0:T(8,128)}), f32[16,192,256]{2,1,0:T(8,128)}, u32[]{:S(2)}, u32[]{:S(2)}) async-start(f32[16,192,256]{2,1,0:T(8,128)} %bitcast.389), calls=%async_computation.9 | async-start | bytes 6291456 | tf_op jit(solution)/shard_map/all_to_all | solution.py:167
  1300.9 70.6 %reduce-scatter.10.cloned.1.call-start = ((), (), s32[]{:S(2)}) async-start(), calls=%async_computation.21 | async-start | bytes 327680
  1311.2 61.8 %reduce-scatter.8.cloned.1.call-start = ((), (), s32[]{:S(2)}) async-start(), calls=%async_computation.20 | async-start | bytes 655360 | tf_op jit(solution)/shard_map/reduce_scatter | solution.py:201
  1311.5 8.2 copy-start.7
  1311.5 8.2 copy-start.11
  1319.7 5.2 copy-start.5
  1325.0 7.7 copy-start.3
  1325.0 7.7 copy-start.9
  1338.7 53.7 %reduce-scatter.6.cloned.1.call-start = ((), (), s32[]{:S(2)}) async-start(), calls=%async_computation.19 | async-start | bytes 655360 | tf_op jit(solution)/shard_map/reduce_scatter | solution.py:200
  1339.0 8.2 copy-start.24
  1339.0 8.2 copy-start.30
  1347.1 5.2 copy-start.28
  1352.3 7.4 copy-start.22
  1352.3 7.4 copy-start.26
  1365.8 6.6 copy-start.85
  1365.8 6.6 copy-start.89
  1365.8 6.6 copy-start.90
  1365.8 7.2 copy-start.44
  1368.9 25.4 %copy-start.66 = (s32[2048]{0:T(1024)S(1)}, s32[2048]{0:T(1024)}, u32[]{:S(2)}) copy-start(s32[2048]{0:T(1024)} %broadcast_clamp_fusion) | copy-start | bytes 24580
  1394.3 8.8 copy-start.64
  1403.1 10.5 copy-start.62
  1413.6 10.6 copy-start.39
  1428.4 9.2 copy-start.38
  (46 other events, 159.7 us)
Sparse Core Ops, SparseCore 0:
  1311.3 25.2 reduce-scatter.9
  1339.7 25.0 reduce-scatter.7
  1367.6 24.7 reduce-scatter.5
where the time goes:
time: 1460 us; the launch traced here: 1450 us
  waiting for transfers between devices  731 us (50%)
  local copies, waits for them, and re-layouts  319 us (22%)
  matrix products  135 us (9%)
  other arithmetic  104 us (7%)
  starting transfers between devices  73.8 us (5%)
  blocking collectives  69.1 us (5%)
  between operations  15.8 us (1%)
    all_to_all x4, waiting for transfers between devices, local(): lax.all_to_all(send_grads, 'expert', split_axis=0, concat_axis=0, tiled=T...  241 us
    all_to_all x4, waiting for transfers between devices, local(): lax.all_to_all(slot_out.reshape(EXPERTS, CAP, DOUT), 'expert', split_axis...  184 us
    all_to_all x4, waiting for transfers between devices, local(): lax.all_to_all(send_rows, 'expert', split_axis=0, concat_axis=0, tiled=True)  169 us
    all_to_all x4, waiting for transfers between devices, local(): lax.all_to_all(slot_back.reshape(EXPERTS, CAP, D), 'expert', split_axis=0...  119 us
    scatter x4, local copies, waits for them, and re-layouts, local(): send_grads = jnp.zeros((EXPERTS * CAP, DOUT), jnp.float32).at[slot_place]...  45.9 us
    scatter x4, local copies, waits for them, and re-layouts, local(): send_rows = jnp.zeros((EXPERTS * CAP, D), jnp.float32).at[slot_place].set...  44.3 us
    psum x1, blocking collectives, local(): gate_grad = lax.psum(gate_local, ('dp', 'expert'))  41.1 us
    gather x4, local copies, waits for them, and re-layouts, local(): returned_back.reshape(EXPERTS * CAP, D)[slot_place]  38.5 us
  transfers between devices with their start and end apart: 19, of which 14 were waited for; matrix products, arithmetic and copies ran while one was open for 33% of the time, Pallas kernels for 0%

commit v1 on v0

v1 whole, which is shorter than its diff:
```python
import functools
import math

import jax
import jax.numpy as jnp
from jax import lax
from jax.experimental import pallas as pl
from jax.experimental.pallas import tpu as pltpu
from jax.sharding import PartitionSpec as P

D = 256
HID = 256
DOUT = 256
EXPERTS = 16
BITS = 4
TASKS = 2
SELECT = 4
PAIRS = TASKS * SELECT
CORES = 2
TILE = 512
PIECES = 4

OFFSET = 3.5
SHARPNESS = 10.0
MOMENTUM = 0.5
AVERAGE_DECAY = 0.5
EXPERT_RATE = 0.4
GATE_RATE = 0.01
F32 = jnp.float32
BF16 = jnp.bfloat16
MESH = pl.DeviceIdType.MESH


def update(weight, gradient, momentum, average, step_rate):
    momentum_new = MOMENTUM * momentum + gradient
    weight_new = weight - step_rate * (gradient + MOMENTUM * momentum_new)
    average_new = AVERAGE_DECAY * average + (1.0 - AVERAGE_DECAY) * weight_new
    return (momentum_new, weight_new, average_new)


def mm(left, right):
    return jnp.dot(left, right, preferred_element_type=F32)


def split2(value):
    high = value.astype(BF16)
    return high, (value - high.astype(F32)).astype(BF16)


def split3(value):
    high = value.astype(BF16)
    rest = value - high.astype(F32)
    middle = rest.astype(BF16)
    return high, middle, (rest - middle.astype(F32)).astype(BF16)


def expert_kernel(
    dims,
    x_hbm,
    cot_hbm,
    routes_ref,
    lengths_ref,
    gw_ref,
    first_hbm,
    second_hbm,
    bias_ref,
    out_hbm,
    ig_hbm,
    gsum_ref,
    gg_ref,
    pack_ref,
    xin,
    cin,
    grb,
    xcat,
    xt,
    ccat,
    ct,
    gm,
    st,
    mt,
    acc,
    iga,
    s_gh,
    s_hc,
    s_w1,
    s_w1t,
    s_w2,
    s_w2t,
    bias,
    b1acc,
    b2grad,
    wbuf,
    gbuf,
    rbuf,
    psum,
    fbuf,
    ret_out,
    ret_ig,
    ret_gc,
    gcp,
    saved,
    ar_own,
    ar_sib,
    ar_dp,
    ar_z,
    local_sem,
    sib_send,
    sib_recv,
    z_send,
    z_recv,
    p_send,
    p_recv,
    a_send,
    a_recv,
    f_send,
    f_recv,
    r_send,
    r_recv,
):
    rows, n_dp, nz, per_device = dims
    count = nz * per_device
    part = D // n_dp
    lanes = 128
    kinds = BITS + 1
    both = CORES * rows
    relay = n_dp == 4
    width = 2 * HID // n_dp
    upper, lower = slice(0, part), slice(part, 2 * part + 8)
    dp = lax.axis_index("dp")
    place = lax.axis_index("expert")
    z = place // CORES
    core = place % CORES
    sibling = (dp, z * CORES + (1 - core))

    def peer(m):
        return ((dp + m) % n_dp, place)

    def plane(dz):
        return (dp, ((z + dz) % nz) * CORES + core)

    flip = (dp // 2) * 2 + (1 - dp % 2)
    turn = (1 - dp // 2) * 2 + dp % 2
    across = (n_dp - 1) - dp

    def slot(k):
        step = k + (per_device - 1)
        return (step // per_device) % nz, step % per_device

    def expert_of(k):
        dz, l = slot(k)
        return (((z + dz) % nz) * CORES + core) * per_device + l

    barrier = pltpu.get_barrier_semaphore()
    greet = [sibling] + [peer(m) for m in range(1, n_dp)] + [plane(dz) for dz in range(1, nz)]
    for other in greet:
        pl.semaphore_signal(barrier, inc=1, device_id=other, device_id_type=MESH)
    copies = [
        pltpu.make_async_copy(x_hbm, xin.at[0], local_sem.at[0]),
        pltpu.make_async_copy(cot_hbm, cin.at[0], local_sem.at[1]),
    ]
    loads = []
    for l in range(per_device):
        loads += [
            pltpu.make_async_copy(first_hbm.at[l], pack_ref.at[l, upper], local_sem.at[2 + 3 * l]),
            pltpu.make_async_copy(
                second_hbm.at[l], pack_ref.at[l, slice(part, 2 * part)], local_sem.at[3 + 3 * l]
            ),
        ]
    for copy in loads + copies:
        copy.start()
    spread_lane = lax.broadcasted_iota(jnp.int32, (1, HID), 1)
    bias_row, bias_lane = dp * width // HID, dp * width % HID
    for l in range(per_device):
        wide = jnp.concatenate([bias_ref[l : l + 1, :]] * (HID // width), axis=1)
        wide = jnp.where((spread_lane >= bias_lane) & (spread_lane < bias_lane + width), wide, 0.0)
        rows_of = lax.broadcasted_iota(jnp.int32, (8, HID), 0)
        pack_ref[l, 2 * part : 2 * part + 8, :] = jnp.where(rows_of == bias_row, wide, 0.0)
    for copy in loads:
        copy.wait()
    pl.semaphore_wait(barrier, len(greet))

    def remote(src, dst, send, recv, where):
        return pltpu.make_async_remote_copy(
            src_ref=src, dst_ref=dst, send_sem=send, recv_sem=recv, device_id=where, device_id_type=MESH
        )

    def spread(k):
        def link(m, source, rows_at, where):
            at = wbuf.at[k, source, rows_at]
            return functools.partial(remote, at, at, p_send.at[k, m], p_recv.at[k, m], where)

        everything = slice(0, 2 * part + 8)
        if relay:
            return [
                link(0, dp, everything, (flip, place)),
                link(1, dp, everything, (turn, place)),
                link(2, flip, upper, (turn, place)),
                link(3, turn, lower, (flip, place)),
            ]
        return [link(m - 1, dp, everything, peer(m)) for m in range(1, n_dp)]

    first_hop = 2 if relay else n_dp - 1

    def along(k):
        dz, l = slot(k)
        return remote(pack_ref.at[l], wbuf.at[k, dp], z_send.at[k], z_recv.at[k], plane(nz - dz))

    def own(k):
        dz, l = slot(k)
        return pltpu.make_async_copy(pack_ref.at[l], wbuf.at[k, dp], local_sem.at[4 + 3 * l])

    last = count - 1
    mine = [k for k in range(count) if slot(k)[0] == 0]

    def forward(k):
        if per_device > 1:

            @pl.when(k == last)
            def _():
                own(last).wait()

            @pl.when(k < last)
            def _():
                along(k).wait_recv()
        else:
            along(k).wait_recv()
        for copy in spread(k)[:first_hop]:
            copy().start()

    def pass_on(k):
        if relay:
            hops = spread(k)
            for copy in hops[:first_hop]:
                copy().wait_recv()
            for copy in hops[first_hop:]:
                copy().start()

    def scatter(k):
        def link(m, quarter, at, rows_at, where):
            return functools.partial(
                remote,
                gbuf.at[k, quarter, rows_at],
                rbuf.at[k, at, rows_at],
                a_send.at[k, m],
                a_recv.at[k, m],
                where,
            )

        if relay:
            return [
                link(0, flip, 0, upper, (flip, place)),
                link(1, across, 1, upper, (flip, place)),
                link(2, turn, 0, lower, (turn, place)),
                link(3, across, 1, lower, (turn, place)),
                link(4, turn, 2, upper, (turn, place)),
                link(5, flip, 2, lower, (flip, place)),
            ]
        everything = slice(0, 2 * part + 8)
        return [
            link(m - 1, (dp + m) % n_dp, m - 1, everything, peer(m)) for m in range(1, n_dp)
        ]

    first_sum = 4 if relay else n_dp - 1

    def add_on(k):
        if relay:
            hops = scatter(k)
            hops[1]().wait_recv()
            hops[3]().wait_recv()
            gbuf[k, turn, upper] = gbuf[k, turn, upper] + rbuf[k, 1, upper]
            gbuf[k, flip, lower] = gbuf[k, flip, lower] + rbuf[k, 1, lower]
            hops[4]().start()
            hops[5]().start()

    def deliver(k):
        dz, l = slot(k)
        return remote(psum.at[k], fbuf.at[dz - 1, l], f_send.at[k], f_recv.at[dz - 1, l], plane(dz))

    def collect(k):
        hops = scatter(k)
        for m in [0, 2, 4, 5] if relay else range(n_dp - 1):
            hops[m]().wait_recv()
        total = gbuf[k, dp]
        for m in [0, 2] if relay else range(n_dp - 1):
            total = total + rbuf[k, m]
        psum[k] = total

    own(0).start()
    own(0).wait()
    for copy in spread(0)[:first_hop]:
        copy().start()
    for k in range(1, count):
        if k in mine:
            own(k).start()
        else:
            along(k).start()
    if per_device > 1:
        forward(jnp.int32(last))
    sends = [
        remote(x_hbm, xin.at[1], sib_send.at[0], sib_recv.at[0], sibling),
        remote(cot_hbm, cin.at[1], sib_send.at[1], sib_recv.at[1], sibling),
        remote(grb.at[0], grb.at[1], sib_send.at[2], sib_recv.at[2], sibling),
    ]
    sends[0].start()
    sends[1].start()

    acc[...] = jnp.zeros_like(acc)
    iga[...] = jnp.zeros_like(iga)

    def prepare(half):
        step = 256

        def body(i, _):
            src = pl.ds(pl.multiple_of(i * step, step), step)
            dst = pl.ds(pl.multiple_of(half * rows + i * step, step), step)
            value = xin[half, src, :]
            high, middle, low = split3(value)
            xcat[dst, 0:D] = low
            xcat[dst, D : 2 * D] = middle
            xcat[dst, 2 * D : 3 * D] = high
            high, low = split2(value.T)
            xt[0:D, dst] = high
            xt[D : 2 * D, dst] = low
            for t in range(TASKS):
                value = cin[half, src, t * DOUT : (t + 1) * DOUT]
                high, low = split2(value)
                base = t * 2 * DOUT
                ccat[dst, base : base + DOUT] = low
                ccat[dst, base + DOUT : base + 2 * DOUT] = high
                high, low = split2(value.T)
                ct[base : base + DOUT, dst] = high
                ct[base + DOUT : base + 2 * DOUT, dst] = low
            return 0

        lax.fori_loop(0, rows // step, body, 0)

    def tables(half):
        chosen = grb[half, PAIRS : 2 * PAIRS, :]
        gates = grb[half, 0:PAIRS, :]
        second = lax.broadcasted_iota(jnp.int32, chosen.shape, 0) >= SELECT
        strengths = []
        tasks = []
        for k in range(count):
            hit = chosen == expert_of(k).astype(F32)
            strengths.append(jnp.sum(jnp.where(hit, gates, 0.0), axis=0, keepdims=True))
            tasks.append(jnp.sum(jnp.where(hit & second, 1.0, 0.0), axis=0, keepdims=True))
        strength = jnp.concatenate(strengths, axis=0)
        task = jnp.concatenate(tasks, axis=0)
        st[:, half * rows : (half + 1) * rows] = strength
        mt[:, half * rows : (half + 1) * rows] = task
        table = jnp.concatenate(
            [strength, task, jnp.zeros((lanes - 2 * count, rows), F32)], axis=0
        )
        gm[half * rows : (half + 1) * rows, :] = table.T

    def mm3(left, right_high, right_low):
        high, low = split2(left)
        return (mm(low, right_high) + mm(high, right_low)) + mm(high, right_high)

    sessions = lengths_ref.shape[1]
    spans = lengths_ref[...].astype(F32)
    square = (sessions, sessions)
    wide = jnp.broadcast_to(spans, square)
    line = lax.broadcasted_iota(jnp.int32, square, 0)
    column = lax.broadcasted_iota(jnp.int32, square, 1)
    begin = jnp.sum(jnp.where(column < line, wide, 0.0), axis=1, keepdims=True)
    span = jnp.sum(jnp.where(column == line, wide, 0.0), axis=1, keepdims=True)
    spot = lax.broadcasted_iota(jnp.int32, (sessions, rows), 1).astype(F32)
    member = jnp.where((spot >= begin) & (spot < begin + span), 1.0, 0.0).astype(BF16)
    gates_t = jnp.concatenate(
        [gw_ref[p * kinds + b : p * kinds + b + 1, :] for b in range(kinds) for p in range(PAIRS)], axis=0
    )

    for copy in copies:
        copy.wait()
    prepare(0)
    sums = mm(member, xcat[0:rows, 0:D]) + mm(member, xcat[0:rows, D : 2 * D])
    sums = sums + mm(member, xcat[0:rows, 2 * D : 3 * D])
    means = sums / span
    m_high, m_low = split2(means.T)
    shift = mm3(gates_t, m_high, m_low)
    s_high, s_low = split2(shift)
    logits = mm3(gates_t, xt[0:D, 0:rows], xt[D : 2 * D, 0:rows])
    logits = logits + (mm(s_low, member) + mm(s_high, member))
    chosen = routes_ref[...]
    weight_logit = logits[0:PAIRS]
    group = lax.broadcasted_iota(jnp.int32, (PAIRS, rows), 0) >= SELECT

    def per_task(value, reduce, neutral):
        first = reduce(jnp.where(group, neutral, value), axis=0, keepdims=True)
        second = reduce(jnp.where(group, value, neutral), axis=0, keepdims=True)
        return jnp.where(group, second, first)

    grown = jnp.exp(weight_logit - per_task(weight_logit, jnp.max, -jnp.inf))
    mix = grown / per_task(grown, jnp.sum, 0.0)
    strength = jnp.ones((PAIRS, rows), F32)
    steps, slopes, signs = [], [], []
    for b in range(BITS):
        bit = lax.shift_right_logical(chosen, jnp.full_like(chosen, b)) & 1
        sign = 2.0 * bit.astype(F32) - 1.0
        raw = sign * logits[(b + 1) * PAIRS : (b + 2) * PAIRS] + OFFSET
        c = jnp.clip(raw, -0.5 * SHARPNESS, 0.5 * SHARPNESS)
        steps.append(-2.0 / SHARPNESS**3 * (c * c * c) + 1.5 / SHARPNESS * c + 0.5)
        inside = (raw >= -0.5 * SHARPNESS) & (raw <= 0.5 * SHARPNESS)
        slope = jnp.where(inside, -6.0 / SHARPNESS**3 * (c * c) + 1.5 / SHARPNESS, 0.0)
        slopes.append(sign * slope)
    strength = (steps[0] * steps[1]) * (steps[2] * steps[3])
    grb[0, 0:PAIRS, :] = mix * strength
    grb[0, PAIRS : 2 * PAIRS, :] = chosen.astype(F32)
    sends[2].start()
    saved[0] = mix
    saved[1] = strength
    rest = [
        steps[1] * (steps[2] * steps[3]),
        steps[0] * (steps[2] * steps[3]),
        steps[3] * (steps[0] * steps[1]),
        steps[2] * (steps[0] * steps[1]),
    ]
    for b in range(BITS):
        saved[2 + b] = mix * rest[b] * slopes[b]
    tables(0)
    pass_on(jnp.int32(0))

    def bias_outputs():
        strength = st[...]
        task = mt[...] > 0.5
        total = jnp.zeros((count, DOUT), F32)
        for t in range(TASKS):
            base = t * 2 * DOUT
            total = total + mm3(
                jnp.where(task if t else ~task, strength, 0.0),
                ccat[:, base + DOUT : base + 2 * DOUT],
                ccat[:, base : base + DOUT],
            )
        b2grad[:, 0, :] = total

    lane = lax.broadcasted_iota(jnp.int32, (TILE, lanes), 1)
    tiles = both // TILE

    give_back = [
        remote(acc.at[pl.ds(rows, rows)], ret_out, sib_send.at[3], sib_recv.at[3], sibling),
        remote(iga.at[pl.ds(rows, rows)], ret_ig, sib_send.at[4], sib_recv.at[4], sibling),
        remote(gcp, ret_gc, sib_send.at[5], sib_recv.at[5], sibling),
    ]

    def tile(k, i):
        turned = (i + (k // last) * (tiles // 2)) % tiles
        rs = pl.ds(pl.multiple_of(turned * TILE, TILE), TILE)
        pre = mm(xcat[rs, :], s_w1[...]) + mm(xcat[rs, D : 3 * D], s_w1[0 : 2 * D])
        pre = pre + mm(xcat[rs, 2 * D : 3 * D], s_w1[0:D])
        pre = pre + bias[k, 0:1, :]
        kept = gm[rs, :]
        table = pltpu.roll(kept, (lanes - k) % lanes, 1)
        gate = table[:, 0:1]
        second = table[:, count : count + 1] > 0.5
        picked = jnp.where(second, ccat[rs, 2 * DOUT : 4 * DOUT], ccat[rs, 0 : 2 * DOUT])
        back = mm(picked, s_w2t[...]) + mm(picked[:, DOUT:], s_w2t[0:DOUT])
        hidden = jnp.maximum(pre, 0.0)
        gated = gate * hidden
        inner = jnp.sum(back * hidden, axis=1, keepdims=True)
        gm[rs, :] = jnp.where(lane == 2 * count + k, inner, kept)
        hidden_cot = jnp.where(pre > 0.0, gate * back, 0.0)
        b1acc[...] = b1acc[...] + jnp.sum(hidden_cot.reshape(TILE // 8, 8, HID), axis=0)
        g_high, g_low = split2(gated)
        h_high, h_low = split2(hidden_cot)
        s_gh[rs, 0:HID] = g_high
        s_gh[rs, HID : 2 * HID] = g_low
        s_hc[rs, 0:HID] = h_high
        s_hc[rs, HID : 2 * HID] = h_low
        out = mm(g_low, s_w2[0:HID]) + mm(g_high, s_w2[HID : 2 * HID]) + mm(g_high, s_w2[0:HID])
        out = out + gate * bias[k, 1:2, :]
        acc[rs, 0:DOUT] = acc[rs, 0:DOUT] + jnp.where(second, 0.0, out)
        acc[rs, DOUT : 2 * DOUT] = acc[rs, DOUT : 2 * DOUT] + jnp.where(second, out, 0.0)
        grad = mm(h_low, s_w1t[0:HID]) + mm(h_high, s_w1t[HID : 2 * HID]) + mm(h_high, s_w1t[0:HID])
        iga[rs, :] = iga[rs, :] + grad

    late = [k for k in range(1, count) if k not in mine]
    schedule = [(2 * n, forward, k) for n, k in enumerate(late)]
    if relay:
        schedule += [(0, pass_on, k) for k in mine if k > 0]
        schedule += [(2 * n + 2, pass_on, k) for n, k in enumerate(late)]

    def slot_body(k, _):
        for copy in spread(k)[(first_hop if relay else 0) :]:
            copy().wait_recv()
        w1 = wbuf[k, :, 0:part, :].reshape(D, HID)
        w2 = wbuf[k, :, part : 2 * part, :].reshape(HID, DOUT)
        high, middle, low = split3(w1)
        s_w1[0:D] = high
        s_w1[D : 2 * D] = middle
        s_w1[2 * D : 3 * D] = low
        high, low = split2(w1.T)
        s_w1t[0:HID] = high
        s_w1t[HID : 2 * HID] = low
        high, low = split2(w2)
        s_w2[0:HID] = high
        s_w2[HID : 2 * HID] = low
        high, low = split2(w2.T)
        s_w2t[0:DOUT] = high
        s_w2t[DOUT : 2 * DOUT] = low
        pieces = wbuf[k, 0, 2 * part : 2 * part + 8, :]
        for m in range(1, n_dp):
            pieces = pieces + wbuf[k, m, 2 * part : 2 * part + 8, :]
        bias[k] = pieces
        b1acc[...] = jnp.zeros_like(b1acc)

        def tile_body(i, _):
            for at, action, which in schedule:

                @pl.when(k * tiles + i == at)
                def _(action=action, which=which):
                    action(jnp.int32(which))

            @pl.when((i == tiles // 2) & (k == 0))
            def _():
                for copy in sends:
                    copy.wait_recv()
                prepare(1)
                tables(1)
                bias_outputs()

            if relay:

                @pl.when((i == tiles // 2) & (k >= 1))
                def _():
                    add_on(k - 1)

            @pl.when((i == tiles // 2) & (k == last))
            def _():
                give_back[0].start()
                give_back[1].start()

            tile(k, i)
            return 0

        lax.fori_loop(0, tiles, tile_body, 0)
        h_high, h_low = s_hc[:, 0:HID], s_hc[:, HID : 2 * HID]
        first_grad = mm(xt[0:D], h_low) + mm(xt[D : 2 * D], h_high) + mm(xt[0:D], h_high)
        gbuf[k, :, 0:part, :] = first_grad.reshape(n_dp, part, HID)
        g_high, g_low = s_gh[:, 0:HID], s_gh[:, HID : 2 * HID]
        second = mt[pl.ds(k, 1), :] > 0.5
        c_high = jnp.where(second, ct[2 * DOUT : 3 * DOUT], ct[0:DOUT])
        c_low = jnp.where(second, ct[3 * DOUT : 4 * DOUT], ct[DOUT : 2 * DOUT])
        second_grad = mm(c_high, g_low) + mm(c_low, g_high) + mm(c_high, g_high)
        gbuf[k, :, part : 2 * part, :] = second_grad.T.reshape(n_dp, part, DOUT)
        sums = jnp.concatenate(
            [jnp.sum(b1acc[...], axis=0, keepdims=True), b2grad[k], jnp.zeros((6, HID), F32)], axis=0
        )
        gbuf[k, :, 2 * part : 2 * part + 8, :] = jnp.broadcast_to(sums[None], (n_dp, 8, HID))
        for copy in scatter(k)[:first_sum]:
            copy().start()

        @pl.when(k >= 1)
        def _():
            collect(k - 1)

        @pl.when(k >= 2)
        def _():
            deliver(k - 1).start()

        return 0

    lax.fori_loop(0, count, slot_body, 0)

    inner = gm[...].T[2 * count : 3 * count]
    b2 = bias[:, 1, :]
    task = mt[...] > 0.5
    added = []
    for t in range(TASKS):
        base = t * 2 * DOUT
        added.append(mm3(b2, ct[base : base + DOUT], ct[base + DOUT : base + 2 * DOUT]))
    inner = inner + jnp.where(task, added[1], added[0])

    def pairs_of(half):
        chosen = grb[half, PAIRS : 2 * PAIRS, :]
        total = jnp.zeros((PAIRS, rows), F32)
        for k in range(count):
            hit = chosen == expert_of(k).astype(F32)
            total = total + jnp.where(hit, inner[k : k + 1, half * rows : (half + 1) * rows], 0.0)
        return total

    gcp[...] = pairs_of(1)
    give_back[2].start()
    own_part = pairs_of(0)
    give_back[2].wait_recv()
    gate_cot = own_part + ret_gc[...]
    mix = saved[0]
    pull = gate_cot * saved[1] * mix
    pulls = [pull - mix * per_task(pull, jnp.sum, 0.0)]
    pulls += [gate_cot * saved[2 + b] for b in range(BITS)]
    cots = jnp.concatenate(pulls, axis=0)
    c_high, c_low = split2(cots)
    gathered = lax.dot_general(
        c_low, member, (((1,), (1,)), ((), ())), preferred_element_type=F32
    ) + lax.dot_general(c_high, member, (((1,), (1,)), ((), ())), preferred_element_type=F32)
    m_high, m_low = split2(means)
    x_high, x_low = xcat[0:rows, 2 * D : 3 * D], xcat[0:rows, D : 2 * D]
    ar_own[...] = (
        (mm(c_low, x_high) + mm(c_high, x_low)) + mm(c_high, x_high) + mm3(gathered, m_high, m_low)
    )
    to_sibling = remote(ar_own, ar_sib, r_send.at[0], r_recv.at[0], sibling)
    to_sibling.start()
    add_on(last)

    def to_peer(m):
        return remote(ar_dp.at[dp], ar_dp.at[dp], r_send.at[m], r_recv.at[m], peer(m))

    def to_plane(dz):
        at = n_dp - 1 + dz
        return remote(ar_z.at[z], ar_z.at[z], r_send.at[at], r_recv.at[at], plane(dz))

    level = gathered / jnp.sum(
        jnp.where(column == line, jnp.broadcast_to(span, square), 0.0), axis=0, keepdims=True
    )
    l_high, l_low = split2(level)
    spread_cots = cots + (mm(l_low, member) + mm(l_high, member))
    flat = jnp.concatenate([spread_cots, jnp.zeros((lanes - PAIRS * kinds, rows), F32)], axis=0)
    f_high, f_low = split2(flat.T)
    g_high, g_low = split2(
        jnp.concatenate([gates_t, jnp.zeros((lanes - PAIRS * kinds, D), F32)], axis=0)
    )
    to_sibling.wait_recv()
    ar_dp[dp] = ar_own[...] + ar_sib[...]
    for m in range(1, n_dp):
        to_peer(m).start()
    iga[0:rows, :] = iga[0:rows, :] + (mm(f_low, g_high) + mm(f_high, g_low) + mm(f_high, g_high))
    collect(last)
    if slot(last)[0] != 0:
        deliver(last).start()
    for m in range(1, n_dp):
        to_peer(m).wait_recv()
    total = ar_dp[0]
    for m in range(1, n_dp):
        total = total + ar_dp[m]
    ar_z[z] = total
    for dz in range(1, nz):
        to_plane(dz).start()
    give_back[0].wait_recv()
    give_back[1].wait_recv()

    def finish(i, _):
        rs = pl.ds(pl.multiple_of(i * 256, 256), 256)
        acc[rs, :] = acc[rs, :] + ret_out[rs, :]
        iga[rs, :] = iga[rs, :] + ret_ig[rs, :]
        return 0

    lax.fori_loop(0, rows // 256, finish, 0)
    results = [
        pltpu.make_async_copy(acc.at[pl.ds(0, rows)], out_hbm, local_sem.at[0]),
        pltpu.make_async_copy(iga.at[pl.ds(0, rows)], ig_hbm, local_sem.at[1]),
    ]
    for copy in results:
        copy.start()
    for l in range(per_device):
        total = psum[mine[-1 - l] if per_device == 1 else [k for k in mine if slot(k)[1] == l][0]]
        for dz in range(1, nz):
            remote(
                psum.at[0], fbuf.at[dz - 1, l], f_send.at[0], f_recv.at[dz - 1, l], plane(dz)
            ).wait_recv()
            total = total + fbuf[dz - 1, l]
        gsum_ref[l] = total
    for dz in range(1, nz):
        to_plane(dz).wait_recv()
    total = ar_z[0]
    for dz in range(1, nz):
        total = total + ar_z[dz]
    gg_ref[...] = jnp.concatenate(
        [total[b * PAIRS + p : b * PAIRS + p + 1] for p in range(PAIRS) for b in range(kinds)], axis=0
    )
    for copy in results:
        copy.wait()

    for copy in sends + give_back + [to_sibling]:
        copy.wait_send()
    for m in range(1, n_dp):
        to_peer(m).wait_send()
    for dz in range(1, nz):
        to_plane(dz).wait_send()

    def drain(k, _):
        for copy in spread(k) + scatter(k):
            copy().wait_send()
        return 0

    lax.fori_loop(0, count, drain, 0)
    own_last = [k for k in mine if k > 0]

    def drain_z(k, _):
        along(k).wait_send()
        deliver(k).wait_send()
        return 0

    lax.fori_loop(1, count - len(own_last), drain_z, 0)


def run_experts(features, cotangent, routes_t, lengths, gates_t, first_weight, second_weight, expert_bias):
    rows = features.shape[0]
    n_dp, n_expert = lax.axis_size("dp"), lax.axis_size("expert")
    nz = n_expert // CORES
    per_device, part, _ = first_weight.shape
    height = 2 * part + 8
    count = nz * per_device
    both = CORES * rows
    heads = PAIRS * (BITS + 1)
    hops = n_dp - 1
    gather_hops, sum_hops = (4, 6) if n_dp == 4 else (hops, hops)
    any_spec = pl.BlockSpec(memory_space=pl.ANY)
    vmem = pl.BlockSpec(memory_space=pltpu.VMEM)
    dma = pltpu.SemaphoreType.DMA
    return pl.pallas_call(
        functools.partial(expert_kernel, (rows, n_dp, nz, per_device)),
        out_shape=(
            jax.ShapeDtypeStruct((rows, TASKS * DOUT), F32),
            jax.ShapeDtypeStruct((rows, D), F32),
            jax.ShapeDtypeStruct((per_device, height, D), F32),
            jax.ShapeDtypeStruct((heads, D), F32),
        ),
        in_specs=[any_spec, any_spec, vmem, vmem, vmem, any_spec, any_spec, vmem],
        out_specs=(any_spec, any_spec, vmem, vmem),
        scratch_shapes=[
            pltpu.VMEM((per_device, height, D), F32),
            pltpu.VMEM((2, rows, D), F32),
            pltpu.VMEM((2, rows, TASKS * DOUT), F32),
            pltpu.VMEM((2, 2 * PAIRS, rows), F32),
            pltpu.VMEM((both, 3 * D), BF16),
            pltpu.VMEM((2 * D, both), BF16),
            pltpu.VMEM((both, 4 * DOUT), BF16),
            pltpu.VMEM((4 * DOUT, both), BF16),
            pltpu.VMEM((both, 128), F32),
            pltpu.VMEM((count, both), F32),
            pltpu.VMEM((count, both), F32),
            pltpu.VMEM((both, TASKS * DOUT), F32),
            pltpu.VMEM((both, D), F32),
            pltpu.VMEM((both, 2 * HID), BF16),
            pltpu.VMEM((both, 2 * HID), BF16),
            pltpu.VMEM((3 * D, HID), BF16),
            pltpu.VMEM((2 * HID, D), BF16),
            pltpu.VMEM((2 * HID, DOUT), BF16),
            pltpu.VMEM((2 * DOUT, HID), BF16),
            pltpu.VMEM((count, 8, HID), F32),
            pltpu.VMEM((8, HID), F32),
            pltpu.VMEM((count, 1, DOUT), F32),
            pltpu.VMEM((count, n_dp, height, D), F32),
            pltpu.VMEM((count, n_dp, height, D), F32),
            pltpu.VMEM((count, hops, height, D), F32),
            pltpu.VMEM((count, height, D), F32),
            pltpu.VMEM((nz - 1, per_device, height, D), F32),
            pltpu.VMEM((rows, TASKS * DOUT), F32),
            pltpu.VMEM((rows, D), F32),
            pltpu.VMEM((PAIRS, rows), F32),
            pltpu.VMEM((PAIRS, rows), F32),
            pltpu.VMEM((2 + BITS, PAIRS, rows), F32),
            pltpu.VMEM((heads, D), F32),
            pltpu.VMEM((heads, D), F32),
            pltpu.VMEM((n_dp, heads, D), F32),
            pltpu.VMEM((nz, heads, D), F32),
            dma((2 + 3 * per_device,)),
            dma((6,)),
            dma((6,)),
            dma((count,)),
            dma((count,)),
            dma((count, gather_hops)),
            dma((count, gather_hops)),
            dma((count, sum_hops)),
            dma((count, sum_hops)),
            dma((count,)),
            dma((nz - 1, per_device)),
            dma((n_dp + nz - 1,)),
            dma((n_dp + nz - 1,)),
        ],
        compiler_params=pltpu.CompilerParams(
            collective_id=0, has_side_effects=True, vmem_limit_bytes=60 << 20
        ),
    )(features, cotangent, routes_t, lengths, gates_t, first_weight, second_weight, expert_bias)


def update_kernel(scale, out_raw, ig_raw, gsum, gg, *refs):
    weights, outs = refs[:12], refs[14:26]
    out_ref, ig_ref = refs[12:14]
    out_held, ig_held, load_sem, store_sem = refs[26:]
    loads, stores = [], []
    for n, (src, held, dst) in enumerate([(out_raw, out_held, out_ref), (ig_raw, ig_held, ig_ref)]):
        step = src.shape[0] // PIECES
        for i in range(PIECES):
            rs = pl.ds(i * step, step)
            loads.append(pltpu.make_async_copy(src.at[rs], held.at[rs], load_sem.at[n, i]))
            stores.append(pltpu.make_async_copy(held.at[rs], dst.at[rs], store_sem.at[n, i]))
    for copy in loads:
        copy.start()
    per_device, part, _ = weights[3].shape
    width = weights[9].shape[1]
    dp = lax.axis_index("dp")
    bias_grad = []
    for l in range(per_device):
        mine = jnp.zeros((1, width), F32)
        for q in range(2 * HID // width):
            row, lane = q * width // HID, q * width % HID
            mine = jnp.where(dp == q, gsum[l, 2 * part + row : 2 * part + row + 1, lane : lane + width], mine)
        bias_grad.append(mine)
    grads = [
        (gg[...], GATE_RATE),
        (gsum[:, 0:part], EXPERT_RATE),
        (gsum[:, part : 2 * part], EXPERT_RATE),
        (jnp.concatenate(bias_grad, axis=0), EXPERT_RATE),
    ]
    for n, (gradient, rate) in enumerate(grads):
        weight, momentum, average = weights[3 * n : 3 * n + 3]
        news = update(weight[...], gradient * scale, momentum[...], average[...], rate)
        for ref, value in zip(outs[3 * n : 3 * n + 3], news):
            ref[...] = value
    for load, store in zip(loads, stores):
        load.wait()
        store.start()
    for copy in stores:
        copy.wait()


def run_updates(scale, out_raw, ig_raw, gsum, gg, weights):
    any_spec = pl.BlockSpec(memory_space=pl.ANY)
    vmem = pl.BlockSpec(memory_space=pltpu.VMEM)
    shapes = [out_raw, ig_raw] + [weights[3 * (n // 3)] for n in range(12)]
    return pl.pallas_call(
        functools.partial(update_kernel, scale),
        out_shape=tuple(jax.ShapeDtypeStruct(array.shape, F32) for array in shapes),
        in_specs=[any_spec, any_spec] + [vmem] * 14,
        out_specs=(any_spec, any_spec) + (vmem,) * 12,
        scratch_shapes=[
            pltpu.VMEM(out_raw.shape, F32),
            pltpu.VMEM(ig_raw.shape, F32),
            pltpu.SemaphoreType.DMA((2, PIECES)),
            pltpu.SemaphoreType.DMA((2, PIECES)),
        ],
    )(out_raw, ig_raw, gsum, gg, *weights)


def local(
    features,
    cotangent,
    routes,
    lengths,
    gate_weight,
    first_weight,
    second_weight,
    expert_bias,
    gate_momentum,
    gate_average,
    first_momentum,
    first_average,
    second_momentum,
    second_average,
    bias_momentum,
    bias_average,
):
    out_raw, ig_raw, gsum, gg = run_experts(
        features, cotangent, routes.T, lengths, gate_weight.T, first_weight, second_weight, expert_bias
    )
    row_count = features.shape[0] * lax.axis_size("dp") * lax.axis_size("expert")
    results = run_updates(
        1.0 / math.sqrt(row_count),
        out_raw,
        ig_raw,
        gsum,
        gg,
        [
            gate_weight.T,
            gate_momentum.T,
            gate_average.T,
            first_weight,
            first_momentum,
            first_average,
            second_weight,
            second_momentum,
            second_average,
            expert_bias,
            bias_momentum,
            bias_average,
        ],
    )
    return (*results[:2], *(value.T for value in results[2:5]), *results[5:])


def solution(mesh):
    rows = P(("dp", "expert"), None)
    weight = P("expert", "dp", None)
    bias = P("expert", "dp")
    return jax.shard_map(
        local,
        mesh=mesh,
        in_specs=(
            rows,
            rows,
            rows,
            rows,
            P(),
            weight,
            weight,
            bias,
            P(),
            P(),
            weight,
            weight,
            weight,
            weight,
            bias,
            bias,
        ),
        out_specs=(
            rows,
            rows,
            P(),
            P(),
            P(),
            weight,
            weight,
            weight,
            weight,
            weight,
            weight,
            bias,
            bias,
            bias,
        ),
        check_vma=False,
    )
```

time: 1460 us -> 129 us (0.09)
  waiting for transfers between devices: 731 us -> 0 us
  local copies, waits for them, and re-layouts: 319 us -> 0 us
  matrix products: 135 us -> 0 us
  Pallas kernels: 0 us -> 128 us
  other arithmetic: 104 us -> 0 us
  starting transfers between devices: 73.8 us -> 0 us
  blocking collectives: 69.1 us -> 0 us
  between operations: 15.8 us -> 0.65 us
    all_to_all x16 -> x0, waiting for transfers between devices: 713 us -> none  [the longest x4 241 us: local(): lax.all_to_all(send_grads, 'expert', split_axis=0, concat_axis=0, tiled=T...]
    dot_general x31 -> x0, matrix products: 135 us -> none  [the longest x4 27.1 us: expert_backward(): jnp.einsum('sjch,sjco->jho', hidden, slot_cot, precision=HIGHEST)]
    pallas_call x0 -> x2, Pallas kernels: none -> 128 us  [the longest x1 122 us: run_experts(): pl.pallas_call(functools.partial(expert_kernel, (rows, n_dp, nz, per_devi...]
    scatter x8 -> x0, local copies, waits for them, and re-layouts: 90.2 us -> none  [the longest x4 45.9 us: local(): send_grads = jnp.zeros((EXPERTS * CAP, DOUT), jnp.float32).at[slot_place]...]
    gather x8 -> x0, local copies, waits for them, and re-layouts: 75.3 us -> none  [the longest x4 38.5 us: local(): returned_back.reshape(EXPERTS * CAP, D)[slot_place]]
    all_to_all x16 -> x0, starting transfers between devices: 73.3 us -> none  [the longest x4 18.6 us: local(): lax.all_to_all(send_grads, 'expert', split_axis=0, concat_axis=0, tiled=T...]
    psum x1 -> x0, blocking collectives: 41.1 us -> none  [local(): gate_grad = lax.psum(gate_local, ('dp', 'expert'))]
    reduce_sum x26 -> x0, other arithmetic: 38.1 us -> none  [the longest x4 12.1 us: local(): jnp.sum(gate_terms[begin:begin + micro_rows].reshape(micro_rows, TASKS, S...]
  transfers between devices with their start and end apart: 19 -> 0, of which waited for: 14 -> 0; matrix products, arithmetic and copies ran while one was open for 33% -> 0% of each run, Pallas kernels for 0% -> 0%
where the time goes in v1:
time: 129 us; the launch traced here: 128 us
  Pallas kernels  128 us (99%)
    pallas_call x1, Pallas kernels, run_experts(): pl.pallas_call(functools.partial(expert_kernel, (rows, n_dp, nz, per_devi...  122 us
    pallas_call x1, Pallas kernels, run_updates(): pl.pallas_call(functools.partial(update_kernel, scale), out_shape=tuple((...  5.19 us

profile of v1, /device:TPU:0, one launch (start us, length us, event | category | flops | bytes accessed | tf_op | source)
XLA Modules:
  0.0 128.3 jit_solution(5632338243050920491)
XLA Ops:
  0.6 122.4 %shard_map.263 = (f32[1024,512]{1,0:T(8,128)}, f32[1024,256]{1,0:T(8,128)}, f32[2,136,256]{2,1,0:T(8,128)}, f32[40,256]{1,0:T(8,128)}) custom-call(f32[1024,256]{1,0:T(8,128)} %x_hbm.1, f32[1024,512]{1,0:T(8,128)} %cot_hbm.1, s32[8,1024]{1,0:T(8,128)} %bitcast.11, s32[1,16]{1,0:T(1,128)} %lengths_ref.1, f32[40,256]{1,0:T(8,128)} %bitcast.7, ...), custom_call_target="tpu_custom_call" | custom-call | tf_op jit(solution)/shard_map/pallas_call | solution.py:711
  123.1 5.2 %shard_map.264 = (f32[1024,512]{1,0:T(8,128)}, f32[1024,256]{1,0:T(8,128)}, f32[40,256]{1,0:T(8,128)}, f32[40,256]{1,0:T(8,128)}, f32[40,256]{1,0:T(8,128)}, /*i...) custom-call(f32[1024,512]{1,0:T(8,128)} %get-tuple-element.32.out_ra, ...), custom_call_target="tpu_custom_call" | custom-call | tf_op jit(solution)/shard_map/pallas_call | solution.py:823

commit v2 on v1

--- a/solution.py
+++ b/solution.py
@@ -17,7 +17,6 @@
 SELECT = 4
 PAIRS = TASKS * SELECT
 CORES = 2
-TILE = 512
 PIECES = 4
 
 OFFSET = 3.5
@@ -91,12 +90,9 @@
     b1acc,
     b2grad,
     wbuf,
-    gbuf,
     rbuf,
     psum,
     fbuf,
-    ret_out,
-    ret_ig,
     ret_gc,
     gcp,
     saved,
@@ -117,6 +113,7 @@
     f_recv,
     r_send,
     r_recv,
+    free_sem,
 ):
     rows, n_dp, nz, per_device = dims
     count = nz * per_device
@@ -125,8 +122,9 @@
     kinds = BITS + 1
     both = CORES * rows
     relay = n_dp == 4
+    tile_rows = rows
     width = 2 * HID // n_dp
-    upper, lower = slice(0, part), slice(part, 2 * part + 8)
+    upper, lower, everything = slice(0, part), slice(part, 2 * part + 8), slice(0, 2 * part + 8)
     dp = lax.axis_index("dp")
     place = lax.axis_index("expert")
     z = place // CORES
@@ -136,20 +134,29 @@
     def peer(m):
         return ((dp + m) % n_dp, place)
 
-    def plane(dz):
-        return (dp, ((z + dz) % nz) * CORES + core)
+    def plane_at(step):
+        total, bit = 0, 1
+        while bit < nz:
+            here, there = (z // bit) % 2, (step // bit) % 2
+            total = total + bit * (here + there - 2 * here * there)
+            bit *= 2
+        return total
+
+    def plane(step):
+        return (dp, plane_at(step) * CORES + core)
 
     flip = (dp // 2) * 2 + (1 - dp % 2)
     turn = (1 - dp // 2) * 2 + dp % 2
     across = (n_dp - 1) - dp
 
     def slot(k):
-        step = k + (per_device - 1)
-        return (step // per_device) % nz, step % per_device
+        turn_of = k + (per_device - 1)
+        step = (turn_of // per_device) % nz
+        return step, turn_of % per_device
 
     def expert_of(k):
         dz, l = slot(k)
-        return (((z + dz) % nz) * CORES + core) * per_device + l
+        return (plane_at(dz) * CORES + core) * per_device + l
 
     barrier = pltpu.get_barrier_semaphore()
     greet = [sibling] + [peer(m) for m in range(1, n_dp)] + [plane(dz) for dz in range(1, nz)]
@@ -190,7 +197,6 @@
             at = wbuf.at[k, source, rows_at]
             return functools.partial(remote, at, at, p_send.at[k, m], p_recv.at[k, m], where)
 
-        everything = slice(0, 2 * part + 8)
         if relay:
             return [
                 link(0, dp, everything, (flip, place)),
@@ -204,7 +210,13 @@
 
     def along(k):
         dz, l = slot(k)
-        return remote(pack_ref.at[l], wbuf.at[k, dp], z_send.at[k], z_recv.at[k], plane(nz - dz))
+        return remote(
+            pack_ref.at[l, everything], wbuf.at[k, dp, everything], z_send.at[k], z_recv.at[k], plane(dz)
+        )
+
+    def assembled(k):
+        for copy in spread(k)[(first_hop if relay else 0) :]:
+            copy().wait_recv()
 
     def own(k):
         dz, l = slot(k)
@@ -240,7 +252,7 @@
         def link(m, quarter, at, rows_at, where):
             return functools.partial(
                 remote,
-                gbuf.at[k, quarter, rows_at],
+                wbuf.at[k, quarter, rows_at],
                 rbuf.at[k, at, rows_at],
                 a_send.at[k, m],
                 a_recv.at[k, m],
@@ -256,7 +268,6 @@
                 link(4, turn, 2, upper, (turn, place)),
                 link(5, flip, 2, lower, (flip, place)),
             ]
-        everything = slice(0, 2 * part + 8)
         return [
             link(m - 1, (dp + m) % n_dp, m - 1, everything, peer(m)) for m in range(1, n_dp)
         ]
@@ -268,20 +279,26 @@
             hops = scatter(k)
             hops[1]().wait_recv()
             hops[3]().wait_recv()
-            gbuf[k, turn, upper] = gbuf[k, turn, upper] + rbuf[k, 1, upper]
-            gbuf[k, flip, lower] = gbuf[k, flip, lower] + rbuf[k, 1, lower]
+            wbuf[k, turn, upper] = wbuf[k, turn, upper] + rbuf[k, 1, upper]
+            wbuf[k, flip, lower] = wbuf[k, flip, lower] + rbuf[k, 1, lower]
             hops[4]().start()
             hops[5]().start()
 
     def deliver(k):
         dz, l = slot(k)
-        return remote(psum.at[k], fbuf.at[dz - 1, l], f_send.at[k], f_recv.at[dz - 1, l], plane(dz))
+        return remote(
+            psum.at[k, everything],
+            fbuf.at[dz - 1, l, everything],
+            f_send.at[k],
+            f_recv.at[dz - 1, l],
+            plane(dz),
+        )
 
     def collect(k):
         hops = scatter(k)
         for m in [0, 2, 4, 5] if relay else range(n_dp - 1):
             hops[m]().wait_recv()
-        total = gbuf[k, dp]
+        total = wbuf[k, dp]
         for m in [0, 2] if relay else range(n_dp - 1):
             total = total + rbuf[k, m]
         psum[k] = total
@@ -290,13 +307,14 @@
     own(0).wait()
     for copy in spread(0)[:first_hop]:
         copy().start()
-    for k in range(1, count):
-        if k in mine:
-            own(k).start()
-        else:
-            along(k).start()
-    if per_device > 1:
-        forward(jnp.int32(last))
+    for k in mine[1:]:
+        own(k).start()
+    late = [k for k in range(1, count) if k not in mine]
+
+    def send_along(k):
+        along(k).start()
+
+    send_along(late[0])
     sends = [
         remote(x_hbm, xin.at[1], sib_send.at[0], sib_recv.at[0], sibling),
         remote(cot_hbm, cin.at[1], sib_send.at[1], sib_recv.at[1], sibling),
@@ -375,6 +393,7 @@
     for copy in copies:
         copy.wait()
     prepare(0)
+    send_along(late[1])
     sums = mm(member, xcat[0:rows, 0:D]) + mm(member, xcat[0:rows, D : 2 * D])
     sums = sums + mm(member, xcat[0:rows, 2 * D : 3 * D])
     means = sums / span
@@ -421,6 +440,8 @@
         saved[2 + b] = mix * rest[b] * slopes[b]
     tables(0)
     pass_on(jnp.int32(0))
+    forward(jnp.int32(1))
+    send_along(late[2])
 
     def bias_outputs():
         strength = st[...]
@@ -435,18 +456,18 @@
             )
         b2grad[:, 0, :] = total
 
-    lane = lax.broadcasted_iota(jnp.int32, (TILE, lanes), 1)
-    tiles = both // TILE
+    lane = lax.broadcasted_iota(jnp.int32, (tile_rows, lanes), 1)
+    tiles = both // tile_rows
 
     give_back = [
-        remote(acc.at[pl.ds(rows, rows)], ret_out, sib_send.at[3], sib_recv.at[3], sibling),
-        remote(iga.at[pl.ds(rows, rows)], ret_ig, sib_send.at[4], sib_recv.at[4], sibling),
+        remote(acc.at[pl.ds(rows, rows)], cin.at[1], sib_send.at[3], sib_recv.at[3], sibling),
+        remote(iga.at[pl.ds(rows, rows)], xin.at[1], sib_send.at[4], sib_recv.at[4], sibling),
         remote(gcp, ret_gc, sib_send.at[5], sib_recv.at[5], sibling),
     ]
 
     def tile(k, i):
         turned = (i + (k // last) * (tiles // 2)) % tiles
-        rs = pl.ds(pl.multiple_of(turned * TILE, TILE), TILE)
+        rs = pl.ds(pl.multiple_of(turned * tile_rows, tile_rows), tile_rows)
         pre = mm(xcat[rs, :], s_w1[...]) + mm(xcat[rs, D : 3 * D], s_w1[0 : 2 * D])
         pre = pre + mm(xcat[rs, 2 * D : 3 * D], s_w1[0:D])
         pre = pre + bias[k, 0:1, :]
@@ -461,7 +482,7 @@
         inner = jnp.sum(back * hidden, axis=1, keepdims=True)
         gm[rs, :] = jnp.where(lane == 2 * count + k, inner, kept)
         hidden_cot = jnp.where(pre > 0.0, gate * back, 0.0)
-        b1acc[...] = b1acc[...] + jnp.sum(hidden_cot.reshape(TILE // 8, 8, HID), axis=0)
+        b1acc[...] = b1acc[...] + jnp.sum(hidden_cot.reshape(tile_rows // 8, 8, HID), axis=0)
         g_high, g_low = split2(gated)
         h_high, h_low = split2(hidden_cot)
         s_gh[rs, 0:HID] = g_high
@@ -475,15 +496,24 @@
         grad = mm(h_low, s_w1t[0:HID]) + mm(h_high, s_w1t[HID : 2 * HID]) + mm(h_high, s_w1t[0:HID])
         iga[rs, :] = iga[rs, :] + grad
 
-    late = [k for k in range(1, count) if k not in mine]
-    schedule = [(2 * n, forward, k) for n, k in enumerate(late)]
-    if relay:
-        schedule += [(0, pass_on, k) for k in mine if k > 0]
-        schedule += [(2 * n + 2, pass_on, k) for n, k in enumerate(late)]
+    def settle(k):
+        collect(k)
+
+        @pl.when(k >= 1)
+        def _():
+            deliver(k).start()
 
     def slot_body(k, _):
-        for copy in spread(k)[(first_hop if relay else 0) :]:
-            copy().wait_recv()
+        assembled(k)
+
+        @pl.when((k >= 1) & (k + 1 < count))
+        def _():
+            pass_on(k + 1)
+
+        @pl.when(k + 4 <= late[-1])
+        def _():
+            send_along(k + 4)
+
         w1 = wbuf[k, :, 0:part, :].reshape(D, HID)
         w2 = wbuf[k, :, part : 2 * part, :].reshape(HID, DOUT)
         high, middle, low = split3(w1)
@@ -499,65 +529,71 @@
         high, low = split2(w2.T)
         s_w2t[0:DOUT] = high
         s_w2t[DOUT : 2 * DOUT] = low
-        pieces = wbuf[k, 0, 2 * part : 2 * part + 8, :]
+        pieces = wbuf[k, 0, 2 * part : 2 * part + 2, :]
         for m in range(1, n_dp):
-            pieces = pieces + wbuf[k, m, 2 * part : 2 * part + 8, :]
-        bias[k] = pieces
+            pieces = pieces + wbuf[k, m, 2 * part : 2 * part + 2, :]
+        bias[k, 0:2] = pieces
         b1acc[...] = jnp.zeros_like(b1acc)
 
         def tile_body(i, _):
-            for at, action, which in schedule:
-
-                @pl.when(k * tiles + i == at)
-                def _(action=action, which=which):
-                    action(jnp.int32(which))
-
-            @pl.when((i == tiles // 2) & (k == 0))
+            @pl.when(i == tiles // 2)
             def _():
-                for copy in sends:
-                    copy.wait_recv()
-                prepare(1)
-                tables(1)
-                bias_outputs()
-
-            if relay:
-
-                @pl.when((i == tiles // 2) & (k >= 1))
+                @pl.when(k == 0)
                 def _():
-                    add_on(k - 1)
-
-            @pl.when((i == tiles // 2) & (k == last))
-            def _():
-                give_back[0].start()
-                give_back[1].start()
+                    for copy in sends:
+                        copy.wait_recv()
+                    prepare(1)
+                    pl.semaphore_signal(free_sem, inc=1, device_id=sibling, device_id_type=MESH)
+                    tables(1)
+                    bias_outputs()
+                    pass_on(jnp.int32(1))
+                    forward(jnp.int32(2))
+                    forward(jnp.int32(3))
+
+                @pl.when((k >= 1) & (k + 3 < count))
+                def _():
+                    forward(k + 3)
+
+                @pl.when(k == last)
+                def _():
+                    pl.semaphore_wait(free_sem, 1)
+                    give_back[0].start()
+                    give_back[1].start()
+
+                @pl.when(k >= 2)
+                def _():
+                    settle(k - 2)
 
             tile(k, i)
             return 0
 
         lax.fori_loop(0, tiles, tile_body, 0)
+
+        @pl.when(k >= 1)
+        def _():
+            add_on(k - 1)
+
+        for copy in spread(k):
+            copy().wait_send()
         h_high, h_low = s_hc[:, 0:HID], s_hc[:, HID : 2 * HID]
         first_grad = mm(xt[0:D], h_low) + mm(xt[D : 2 * D], h_high) + mm(xt[0:D], h_high)
-        gbuf[k, :, 0:part, :] = first_grad.reshape(n_dp, part, HID)
+        wbuf[k, :, 0:part, :] = first_grad.reshape(n_dp, part, HID)
         g_high, g_low = s_gh[:, 0:HID], s_gh[:, HID : 2 * HID]
         second = mt[pl.ds(k, 1), :] > 0.5
         c_high = jnp.where(second, ct[2 * DOUT : 3 * DOUT], ct[0:DOUT])
         c_low = jnp.where(second, ct[3 * DOUT : 4 * DOUT], ct[DOUT : 2 * DOUT])
         second_grad = mm(c_high, g_low) + mm(c_low, g_high) + mm(c_high, g_high)
-        gbuf[k, :, part : 2 * part, :] = second_grad.T.reshape(n_dp, part, DOUT)
+        wbuf[k, :, part : 2 * part, :] = second_grad.T.reshape(n_dp, part, DOUT)
         sums = jnp.concatenate(
             [jnp.sum(b1acc[...], axis=0, keepdims=True), b2grad[k], jnp.zeros((6, HID), F32)], axis=0
         )
-        gbuf[k, :, 2 * part : 2 * part + 8, :] = jnp.broadcast_to(sums[None], (n_dp, 8, HID))
+        wbuf[k, :, 2 * part : 2 * part + 8, :] = jnp.broadcast_to(sums[None], (n_dp, 8, HID))
         for copy in scatter(k)[:first_sum]:
             copy().start()
 
-        @pl.when(k >= 1)
+        @pl.when(k == last)
         def _():
-            collect(k - 1)
-
-        @pl.when(k >= 2)
-        def _():
-            deliver(k - 1).start()
+            settle(k - 1)
 
         return 0
 
@@ -583,6 +619,19 @@
     gcp[...] = pairs_of(1)
     give_back[2].start()
     own_part = pairs_of(0)
+    give_back[0].wait_recv()
+
+    def finish_out(i, _):
+        rs = pl.ds(pl.multiple_of(i * 256, 256), 256)
+        acc[rs, :] = acc[rs, :] + cin[1, rs, :]
+        return 0
+
+    lax.fori_loop(0, rows // 256, finish_out, 0)
+    results = [
+        pltpu.make_async_copy(acc.at[pl.ds(0, rows)], out_hbm, local_sem.at[0]),
+        pltpu.make_async_copy(iga.at[pl.ds(0, rows)], ig_hbm, local_sem.at[1]),
+    ]
+    results[0].start()
     give_back[2].wait_recv()
     gate_cot = own_part + ret_gc[...]
     mix = saved[0]
@@ -624,7 +673,10 @@
     ar_dp[dp] = ar_own[...] + ar_sib[...]
     for m in range(1, n_dp):
         to_peer(m).start()
-    iga[0:rows, :] = iga[0:rows, :] + (mm(f_low, g_high) + mm(f_high, g_low) + mm(f_high, g_high))
+    give_back[1].wait_recv()
+    from_gate = mm(f_low, g_high) + mm(f_high, g_low) + mm(f_high, g_high)
+    iga[0:rows, :] = (iga[0:rows, :] + xin[1]) + from_gate
+    results[1].start()
     collect(last)
     if slot(last)[0] != 0:
         deliver(last).start()
@@ -636,28 +688,11 @@
     ar_z[z] = total
     for dz in range(1, nz):
         to_plane(dz).start()
-    give_back[0].wait_recv()
-    give_back[1].wait_recv()
-
-    def finish(i, _):
-        rs = pl.ds(pl.multiple_of(i * 256, 256), 256)
-        acc[rs, :] = acc[rs, :] + ret_out[rs, :]
-        iga[rs, :] = iga[rs, :] + ret_ig[rs, :]
-        return 0
-
-    lax.fori_loop(0, rows // 256, finish, 0)
-    results = [
-        pltpu.make_async_copy(acc.at[pl.ds(0, rows)], out_hbm, local_sem.at[0]),
-        pltpu.make_async_copy(iga.at[pl.ds(0, rows)], ig_hbm, local_sem.at[1]),
-    ]
-    for copy in results:
-        copy.start()
     for l in range(per_device):
         total = psum[mine[-1 - l] if per_device == 1 else [k for k in mine if slot(k)[1] == l][0]]
         for dz in range(1, nz):
-            remote(
-                psum.at[0], fbuf.at[dz - 1, l], f_send.at[0], f_recv.at[dz - 1, l], plane(dz)
-            ).wait_recv()
+            held = fbuf.at[dz - 1, l, everything]
+            remote(psum.at[0, everything], held, f_send.at[0], f_recv.at[dz - 1, l], plane(dz)).wait_recv()
             total = total + fbuf[dz - 1, l]
         gsum_ref[l] = total
     for dz in range(1, nz):
@@ -679,19 +714,18 @@
         to_plane(dz).wait_send()
 
     def drain(k, _):
-        for copy in spread(k) + scatter(k):
+        for copy in scatter(k):
             copy().wait_send()
         return 0
 
     lax.fori_loop(0, count, drain, 0)
-    own_last = [k for k in mine if k > 0]
 
     def drain_z(k, _):
         along(k).wait_send()
         deliver(k).wait_send()
         return 0
 
-    lax.fori_loop(1, count - len(own_last), drain_z, 0)
+    lax.fori_loop(1, late[-1] + 1, drain_z, 0)
 
 
 def run_experts(features, cotangent, routes_t, lengths, gates_t, first_weight, second_weight, expert_bias):
@@ -742,12 +776,9 @@
             pltpu.VMEM((8, HID), F32),
             pltpu.VMEM((count, 1, DOUT), F32),
             pltpu.VMEM((count, n_dp, height, D), F32),
-            pltpu.VMEM((count, n_dp, height, D), F32),
             pltpu.VMEM((count, hops, height, D), F32),
             pltpu.VMEM((count, height, D), F32),
             pltpu.VMEM((nz - 1, per_device, height, D), F32),
-            pltpu.VMEM((rows, TASKS * DOUT), F32),
-            pltpu.VMEM((rows, D), F32),
             pltpu.VMEM((PAIRS, rows), F32),
             pltpu.VMEM((PAIRS, rows), F32),
             pltpu.VMEM((2 + BITS, PAIRS, rows), F32),
@@ -768,6 +799,7 @@
             dma((nz - 1, per_device)),
             dma((n_dp + nz - 1,)),
             dma((n_dp + nz - 1,)),
+            pltpu.SemaphoreType.REGULAR,
         ],
         compiler_params=pltpu.CompilerParams(
             collective_id=0, has_side_effects=True, vmem_limit_bytes=60 << 20

time: 129 us -> 109 us (0.84)
  Pallas kernels: 128 us -> 108 us
    pallas_call x1, Pallas kernels: 122 us -> 103 us  [run_experts(): pl.pallas_call(functools.partial(expert_kernel, (rows, n_dp, nz, per_devi...]
where the time goes in v2:
time: 109 us
  Pallas kernels  108 us (99%)
    pallas_call x1, Pallas kernels, run_experts(): pl.pallas_call(functools.partial(expert_kernel, (rows, n_dp, nz, per_devi...  103 us
    pallas_call x1, Pallas kernels, run_updates(): pl.pallas_call(functools.partial(update_kernel, scale), out_shape=tuple((...  5.19 us

profile of v2, /device:TPU:0, one launch (start us, length us, event | category | flops | bytes accessed | tf_op | source)
XLA Modules:
  0.0 108.6 jit_solution(707581961743046254)
XLA Ops:
  0.6 102.8 %shard_map.263 = (f32[1024,512]{1,0:T(8,128)}, f32[1024,256]{1,0:T(8,128)}, f32[2,136,256]{2,1,0:T(8,128)}, f32[40,256]{1,0:T(8,128)}) custom-call(f32[1024,256]{1,0:T(8,128)} %x_hbm.1, f32[1024,512]{1,0:T(8,128)} %cot_hbm.1, s32[8,1024]{1,0:T(8,128)} %bitcast.11, s32[1,16]{1,0:T(1,128)} %lengths_ref.1, f32[40,256]{1,0:T(8,128)} %bitcast.7, ...), custom_call_target="tpu_custom_call" | custom-call | tf_op jit(solution)/shard_map/pallas_call | solution.py:745
  103.4 5.2 %shard_map.264 = (f32[1024,512]{1,0:T(8,128)}, f32[1024,256]{1,0:T(8,128)}, f32[40,256]{1,0:T(8,128)}, f32[40,256]{1,0:T(8,128)}, f32[40,256]{1,0:T(8,128)}, /*i...) custom-call(f32[1024,512]{1,0:T(8,128)} %get-tuple-element.32.out_ra, ...), custom_call_target="tpu_custom_call" | custom-call | tf_op jit(solution)/shard_map/pallas_call | solution.py:855
